TPU v7x, 32 devices: a whole 2x2x4 slice. The times are simulated.
32 devices in a mesh: lat: 4 (over y, x), lon: 8 (over z, core).
Axes of the slice: x: 2, y: 2, z: 4, core: 2. Of those that a mesh axis runs over, the one named last changes fastest.
Arguments:
- inputs: bfloat16 [360, 360, 256], P('lat', 'lon'), may hold values from -6 to 6
- kernel: bfloat16 [3, 3, 256, 256], replicated, may hold values from -0.125 to 0.125
- cotangent: bfloat16 [360, 360, 256], P('lat', 'lon'), may hold values from -6 to 6
Outputs:
- outputs: bfloat16 [360, 360, 256], P('lat', 'lon')
- input_grad: bfloat16 [360, 360, 256], P('lat', 'lon')
- kernel_grad: float32 [3, 3, 256, 256], replicated
All inputs are finite; a program needn't handle non-finite values.
Results may differ from a plain program's by a relative error of at most 0.001.
Values may be sent and summed in bfloat16 or wider, within the bound.
No kernel may reach another device: no remote copies, remote signals or barrier semaphores. Data moves between devices by JAX's collectives and lax.ppermute only.
A program may use at most 192 MiB of HBM per device.

v0:
```python
import math
import jax
import jax.numpy as jnp
from jax import lax
from jax.sharding import PartitionSpec as P


def with_halo(cells, sides, width):
    for axis, dim in sides:
        count = lax.axis_size(axis)
        head = lax.slice_in_dim(cells, 0, width, axis=dim)
        tail = lax.slice_in_dim(cells, cells.shape[dim] - width, cells.shape[dim], axis=dim)
        cells = jnp.concatenate(
            [
                lax.ppermute(tail, axis, [(i, (i + 1) % count) for i in range(count)]),
                cells,
                lax.ppermute(head, axis, [((i + 1) % count, i) for i in range(count)]),
            ],
            axis=dim,
        )
    return cells


def from_behind(value, axis, steps):
    count = lax.axis_size(axis)
    pairs = [(source, (source + steps) % count) for source in range(count)]
    return lax.ppermute(value, axis, pairs)


def patches(padded, rows, cols):
    pieces = [
        padded[row_tap : row_tap + rows, col_tap : col_tap + cols]
        for row_tap in range(3)
        for col_tap in range(3)
    ]
    return jnp.concatenate(pieces, axis=-1).reshape(rows * cols, -1)


def surround(field):
    return with_halo(field, (("lat", 0), ("lon", 1)), 1)


def polar(padded):
    both = jnp.stack([padded[1], padded[-2]])
    moved = from_behind(both, "lon", lax.axis_size("lon") // 2)
    return (moved[0], moved[1])


def edge_term(row_data, weights, cols, width):
    stacked = jnp.concatenate([row_data[offset : offset + cols] for offset in range(3)], axis=-1)
    return jnp.dot(stacked, weights.reshape(-1, width), preferred_element_type=jnp.float32)


def local(inputs, kernel, cotangent):
    rows, cols, width = inputs.shape
    north = lax.axis_index("lat") == 0
    south = lax.axis_index("lat") == lax.axis_size("lat") - 1
    padded = surround(inputs)
    top, bottom = polar(padded)
    padded = jnp.concatenate(
        [
            jnp.where(north, top, padded[0])[None],
            padded[1:-1],
            jnp.where(south, bottom, padded[-1])[None],
        ],
        0,
    )
    columns = patches(padded, rows, cols)
    outputs = jnp.dot(columns, kernel.reshape(-1, width), preferred_element_type=jnp.float32)
    outputs = outputs.reshape(rows, cols, width).astype(jnp.bfloat16)
    flat_grad = cotangent.reshape(-1, width)
    local_grad = lax.dot_general(
        columns, flat_grad, (((0,), (0,)), ((), ())), preferred_element_type=jnp.float32
    )
    local_grad = local_grad.reshape(3, 3, width, width)
    padded_grad = surround(cotangent)
    grad_top, grad_bottom = polar(padded_grad)
    empty_row = jnp.zeros_like(padded_grad[0])
    padded_grad = jnp.concatenate(
        [
            jnp.where(north, empty_row, padded_grad[0])[None],
            padded_grad[1:-1],
            jnp.where(south, empty_row, padded_grad[-1])[None],
        ],
        0,
    )
    flipped = jnp.transpose(kernel[::-1, ::-1], (0, 1, 3, 2))
    input_grad = jnp.dot(
        patches(padded_grad, rows, cols),
        flipped.reshape(-1, width),
        preferred_element_type=jnp.float32,
    )
    input_grad = input_grad.reshape(rows, cols, width)
    north_term = edge_term(grad_top, flipped[2], cols, width)
    south_term = edge_term(grad_bottom, flipped[0], cols, width)
    input_grad = input_grad.at[0].add(jnp.where(north, north_term, 0.0))
    input_grad = input_grad.at[-1].add(jnp.where(south, south_term, 0.0))
    factor = 1.0 / math.sqrt(rows * cols * lax.axis_size("lat") * lax.axis_size("lon"))
    partial_sum = lax.psum(local_grad, "lon")
    summed = lax.psum(partial_sum, "lat")
    return (outputs, input_grad.astype(jnp.bfloat16), summed * factor)


def solution(mesh):
    in_specs = (P("lat", "lon", None), P(), P("lat", "lon", None))
    out_specs = (P("lat", "lon", None), P("lat", "lon", None), P())
    return jax.shard_map(local, mesh=mesh, in_specs=in_specs, out_specs=out_specs, check_vma=False)
```

profile of v0, /device:TPU:0, one launch (start us, length us, event | category | flops | bytes accessed | tf_op | source)
XLA Modules:
  0.0 271.3 jit_solution(15557798716294932809)
XLA Ops:
  7.2 0.0 all-reduce.3.cloned.1.call-start
  7.2 0.8 fusion.70
  8.0 3.9 %collective-permute-start.1 = (bf16[1,45,256]{2,1,0:T(8,128)(2,1)S(1)}, bf16[1,45,256]{2,1,0:T(8,128)(2,1)S(1)}, u32[]{:S(2)}, u32[]{:S(2)}) collective-permute-start(bf16[1,45,256]{2,1,0:T(8,128)(2,1)S(1)} %get-tuple-element.37), channel_id=1, source_target_pairs={{8,0},{16,8},{24,16},{0,24},{9,1},{17,9},{25,17},{1,25},{10,2},{18... | collective-permute-start | bytes 69128 | tf_op jit(solution)/shard_map/ppermute | solution.py:17
  11.9 1.4 fusion.69
  13.3 2.9 %collective-permute-start.6 = (bf16[1,45,256]{2,1,0:T(8,128)(2,1)}, bf16[1,45,256]{2,1,0:T(8,128)(2,1)S(1)}, u32[]{:S(2)}, u32[]{:S(2)}) collective-permute-start(bf16[1,45,256]{2,1,0:T(8,128)(2,1)} %get-tuple-element.35), channel_id=1, source_target_pairs={{8,0},{16,8},{24,16},{0,24},{9,1},{17,9},{25,17},{1,25},{10,2},{18... | collective-permute-start | bytes 69128 | tf_op jit(solution)/shard_map/ppermute | solution.py:17
  16.2 0.0 collective-permute-start.5
  16.2 1.6 copy.6
  17.8 0.1 reverse_bitcast_fusion
  17.9 0.0 copy-start.2
  17.9 0.9 fusion.71
  18.8 1.1 rev.3
  19.9 1.9 reshape.103
  21.8 0.0 collective-permute-done.5
  21.8 0.1 constant_dynamic-update-slice_fusion.5
  22.0 0.1 fusion.67
  22.2 0.1 collective-permute-start.7
  22.2 3.5 %collective-permute-start.8 = (bf16[92,1,256]{2,1,0:T(2,128)(2,1)S(1)}, bf16[92,1,256]{2,1,0:T(2,128)(2,1)S(1)}, u32[]{:S(2)}, u32[]{:S(2)}) collective-permute-start(bf16[92,1,256]{2,1,0:T(2,128)(2,1)S(1)} %get-tuple-element.32), channel_id=1, source_target_pairs={{1,0},{2,1},{3,2},{4,3},{5,4},{6,5},{7,6},{0,7},{9,8},{10,9},{11,1... | collective-permute-start | bytes 141320 | tf_op jit(solution)/shard_map/ppermute | solution.py:17
  25.8 0.0 collective-permute-done
  25.8 0.1 constant_dynamic-update-slice_fusion.1
  26.0 0.1 fusion.68
  26.1 0.1 collective-permute-start.2
  26.2 3.5 %collective-permute-start.3 = (bf16[92,1,256]{2,1,0:T(2,128)(2,1)S(1)}, bf16[92,1,256]{2,1,0:T(2,128)(2,1)S(1)}, u32[]{:S(2)}, u32[]{:S(2)}) collective-permute-start(bf16[92,1,256]{2,1,0:T(2,128)(2,1)S(1)} %get-tuple-element.34), channel_id=1, source_target_pairs={{1,0},{2,1},{3,2},{4,3},{5,4},{6,5},{7,6},{0,7},{9,8},{10,9},{11,1... | collective-permute-start | bytes 141320 | tf_op jit(solution)/shard_map/ppermute | solution.py:17
  29.7 0.0 collective-permute-done.7
  29.7 0.0 collective-permute-done.8
  29.8 0.1 collective-permute-start.9
  29.8 2.6 collective-permute-done.2
  32.4 0.4 collective-permute-start.4
  32.8 1.6 pad_maximum_fusion.1
  34.4 0.1 slice.295
  34.6 1.6 fusion.7
  36.2 2.8 %fusion.5 = bf16[90,45,2304]{2,1,0:T(8,128)(2,1)} fusion(bf16[90,45,2304]{2,1,0:T(8,128)(2,1)} %fusion.7, bf16[1,47,256]{2,1,0:T(8,128)(2,1)S(1)} %get-tuple-element.30, bf16[90,47,256]{2,1,0:T(8,128)(2,1)S(1)} %slice.295), kind=kLoop, calls=%fused_computation.15 | loop fusion | flops 4147200 | bytes 4401664
  39.0 1.6 pad_maximum_fusion
  40.5 0.1 slice.283
  40.7 1.7 fusion.15
  42.5 2.7 %fusion.13 = bf16[90,45,2304]{2,1,0:T(8,128)(2,1)} fusion(bf16[90,45,2304]{2,1,0:T(8,128)(2,1)} %fusion.15, bf16[1,47,256]{2,1,0:T(8,128)(2,1)S(1)} %get-tuple-element.28, bf16[90,47,256]{2,1,0:T(8,128)(2,1)S(1)} %slice.283), kind=kLoop, calls=%fused_computation.23 | loop fusion | flops 4147200 | bytes 4401664
  45.2 2.8 %fusion.23 = bf16[90,45,2304]{2,1,0:T(8,128)(2,1)} fusion(bf16[90,45,2304]{2,1,0:T(8,128)(2,1)} %fusion.13, bf16[90,47,256]{2,1,0:T(8,128)(2,1)S(1)} %slice.283, bf16[1,47,256]{2,1,0:T(8,128)(2,1)S(1)} %get-tuple-element.28), kind=kLoop, calls=%fused_computation.41 | loop fusion | flops 4147200 | bytes 4401664
  48.0 2.9 %fusion.22 = bf16[90,45,2304]{2,1,0:T(8,128)(2,1)} fusion(bf16[90,45,2304]{2,1,0:T(8,128)(2,1)} %fusion.23, bf16[92,45,256]{2,1,0:T(8,128)(2,1)S(1)} %constant_dynamic-update-slice_fusion, bf16[92,1,256]{2,1,0:T(2,128)(2,1)S(1)} %collective-permute-done.2), kind=kLoop, calls=%fused_computation.39 | loop fusion | flops 4147200 | bytes 4378624
  50.8 1.7 constant_dynamic-update-slice_fusion.3
  52.5 3.1 %fusion.21 = bf16[90,45,2304]{2,1,0:T(8,128)(2,1)} fusion(bf16[90,45,2304]{2,1,0:T(8,128)(2,1)} %constant_dynamic-update-slice_fusion.3, bf16[92,1,256]{2,1,0:T(2,128)(2,1)S(1)} %collective-permute-done.3, bf16[92,45,256]{2,1,0:T(8,128)(2,1)S(1)} %constant_dynamic-update-slice_fusion), kind=kLoop, calls=%fused_computation.37 | loop fusion | flops 4147200 | bytes 4378624
  55.6 1.7 fusion.11
  57.3 2.8 %fusion.9 = bf16[90,45,2304]{2,1,0:T(8,128)(2,1)} fusion(bf16[90,45,2304]{2,1,0:T(8,128)(2,1)} %fusion.11, bf16[1,47,256]{2,1,0:T(8,128)(2,1)S(1)} %get-tuple-element.27, bf16[90,47,256]{2,1,0:T(8,128)(2,1)S(1)} %slice.283), kind=kLoop, calls=%fused_computation.19 | loop fusion | flops 4147200 | bytes 4401664
  60.0 3.1 %fusion.20 = bf16[90,45,2304]{2,1,0:T(8,128)(2,1)} fusion(bf16[90,45,2304]{2,1,0:T(8,128)(2,1)} %fusion.9, bf16[1,47,256]{2,1,0:T(8,128)(2,1)S(1)} %get-tuple-element.27, bf16[90,47,256]{2,1,0:T(8,128)(2,1)S(1)} %slice.283), kind=kLoop, calls=%fused_computation.35 | loop fusion | flops 4147200 | bytes 4401664 | tf_op jit(solution)/shard_map/concatenate | solution.py:36
  63.2 19.5 %reshape.99 = bf16[4050,2304]{1,0:T(8,128)(2,1)} reshape(bf16[90,45,2304]{2,1,0:T(8,128)(2,1)} %fusion.20) | data formatting | bytes 37324800 | tf_op jit(solution)/shard_map/reshape | solution.py:36
  82.7 23.0 %copy.7 = bf16[4050,2304]{0,1:T(8,128)(2,1)} copy(bf16[4050,2304]{1,0:T(8,128)(2,1)} %reshape.99) | data formatting | bytes 37324800 | tf_op jit(solution)/shard_map/reshape | solution.py:36
  105.7 10.6 %fusion.24 = f32[3,3,256,256]{3,2,1,0:T(8,128)} fusion(bf16[3,3,256,4050]{3,2,1,0:T(8,128)(2,1)} %bitcast.46, bf16[4050,256,1,1]{1,0,2,3:T(8,128)(2,1)} %reshape.103), kind=kOutput, calls=%fused_computation.42 | convolution fusion | flops 4777574400 | bytes 23095296 | tf_op jit(solution)/shard_map/dot_general | solution.py:72
  116.3 0.0 all-reduce.3.cloned.1.call-update
  116.3 0.0 all-reduce.5.cloned.1.call-start
  116.4 2.7 fusion.19
  119.1 2.8 %fusion.18 = bf16[90,45,2304]{2,1,0:T(8,128)(2,1)} fusion(bf16[90,45,2304]{2,1,0:T(8,128)(2,1)} %fusion.19, bf16[92,45,256]{2,1,0:T(8,128)(2,1)S(1)} %copy-done.1, bf16[92,1,256]{2,1,0:T(2,128)(2,1)S(1)} %collective-permute-done.7), kind=kLoop, calls=%fused_computation.31 | loop fusion | flops 4147200 | bytes 4378624
  121.9 1.6 constant_dynamic-update-slice_fusion.7
  123.4 2.9 %fusion.17 = bf16[90,45,2304]{2,1,0:T(8,128)(2,1)} fusion(bf16[90,45,2304]{2,1,0:T(8,128)(2,1)} %constant_dynamic-update-slice_fusion.7, bf16[92,1,256]{2,1,0:T(2,128)(2,1)S(1)} %collective-permute-done.8, bf16[92,45,256]{2,1,0:T(8,128)(2,1)S(1)} %copy-done.1), kind=kLoop, calls=%fused_computation.29 | loop fusion | flops 4147200 | bytes 4378624
  126.4 1.6 fusion.3
  127.9 2.7 %fusion.1 = bf16[90,45,2304]{2,1,0:T(8,128)(2,1)} fusion(bf16[90,45,2304]{2,1,0:T(8,128)(2,1)} %fusion.3, bf16[1,47,256]{2,1,0:T(8,128)(2,1)S(1)} %get-tuple-element.29, bf16[90,47,256]{2,1,0:T(8,128)(2,1)S(1)} %slice.295), kind=kLoop, calls=%fused_computation.11 | loop fusion | flops 4147200 | bytes 4401664
  130.7 2.7 fusion.16
  133.4 51.7 %all-reduce.3.cloned.1.call-done = f32[3,3,256,256]{3,2,1,0:T(8,128)} async-done(((f32[3,3,256,256]{3,2,1,0:T(8,128)}), f32[3,3,256,256]{3,2,1,0:T(8,128)}) %all-reduce.3.cloned.1.call-update) | async-done | bytes 2359312 | tf_op jit(solution)/shard_map/psum | solution.py:99
  185.1 0.0 all-reduce.5.cloned.1.call-update
  185.2 9.9 %fusion.72 = f32[90,45,256]{2,1,0:T(8,128)S(1)} fusion(bf16[90,45,2304]{2,1,0:T(8,128)(2,1)} %fusion.16, bf16[2304,256,1]{1,0,2:T(8,128)(2,1)S(1)} %bitcast.50), kind=kOutput, calls=%fused_computation.114 | convolution fusion | flops 4777574400 | bytes 23989248 | tf_op jit(solution)/shard_map/dot_general | solution.py:88
  195.1 0.2 fusion.62
  195.3 0.2 fusion.28
  195.5 0.0 copy-start.7
  195.6 1.6 convert_element_type.7
  197.2 11.6 %convolution_convert_fusion = bf16[90,45,256]{2,1,0:T(8,128)(2,1)} fusion(bf16[90,45,2304]{2,1,0:T(8,128)(2,1)} %fusion.20, bf16[2304,256,1]{1,0,2:T(8,128)(2,1)S(1)} %bitcast.49), kind=kOutput, calls=%fused_computation.44 | convolution fusion | flops 4778611200 | bytes 21915648 | tf_op jit(solution)/shard_map/dot_general | solution.py:69
  208.8 52.4 %all-reduce.5.cloned.1.call-done = f32[3,3,256,256]{3,2,1,0:T(8,128)} async-done(((f32[3,3,256,256]{3,2,1,0:T(8,128)}), f32[3,3,256,256]{3,2,1,0:T(8,128)}) %all-reduce.5.cloned.1.call-update) | async-done | bytes 2359312 | tf_op jit(solution)/shard_map/psum | solution.py:100
  261.2 3.3 %broadcast_multiply_fusion = f32[3,3,256,256]{3,2,1,0:T(8,128)} fusion(f32[3,3,256,256]{3,2,1,0:T(8,128)} %all-reduce.5.cloned.1.call-done), kind=kLoop, calls=%fused_computation.45 | loop fusion | flops 589824 | bytes 4718592 | tf_op jit(solution)/shard_map/mul | solution.py:101
  (31 shorter events, 0.2 us)
Async XLA Ops:
  7.2 178.0 %all-reduce.3.cloned.1.call-start = ((), (), s32[]{:S(2)}) async-start(), calls=%async_computation | async-start | bytes 4718592 | tf_op jit(solution)/shard_map/psum | solution.py:99
  8.0 18.0 %collective-permute-start.1 = (bf16[1,45,256]{2,1,0:T(8,128)(2,1)S(1)}, bf16[1,45,256]{2,1,0:T(8,128)(2,1)S(1)}, u32[]{:S(2)}, u32[]{:S(2)}) collective-permute-start(bf16[1,45,256]{2,1,0:T(8,128)(2,1)S(1)} %get-tuple-element.37), channel_id=1, source_target_pairs={{8,0},{16,8},{24,16},{0,24},{9,1},{17,9},{25,17},{1,25},{10,2},{18... | collective-permute-start | bytes 69128 | tf_op jit(solution)/shard_map/ppermute | solution.py:17
  11.9 13.9 %collective-permute-start = (bf16[1,45,256]{2,1,0:T(8,128)(2,1)S(1)}, bf16[1,45,256]{2,1,0:T(8,128)(2,1)S(1)}, u32[]{:S(2)}, u32[]{:S(2)}) collective-permute-start(bf16[1,45,256]{2,1,0:T(8,128)(2,1)S(1)} %get-tuple-element.38), channel_id=1, source_target_pairs={{0,8},{8,16},{16,24},{24,0},{1,9},{9,17},{17,25},{25,1},{2,10},{10... | collective-permute-start | bytes 69128 | tf_op jit(solution)/shard_map/ppermute | solution.py:15
  13.3 8.7 %collective-permute-start.6 = (bf16[1,45,256]{2,1,0:T(8,128)(2,1)}, bf16[1,45,256]{2,1,0:T(8,128)(2,1)S(1)}, u32[]{:S(2)}, u32[]{:S(2)}) collective-permute-start(bf16[1,45,256]{2,1,0:T(8,128)(2,1)} %get-tuple-element.35), channel_id=1, source_target_pairs={{8,0},{16,8},{24,16},{0,24},{9,1},{17,9},{25,17},{1,25},{10,2},{18... | collective-permute-start | bytes 69128 | tf_op jit(solution)/shard_map/ppermute | solution.py:17
  16.2 5.6 %collective-permute-start.5 = (bf16[1,45,256]{2,1,0:T(8,128)(2,1)}, bf16[1,45,256]{2,1,0:T(8,128)(2,1)S(1)}, u32[]{:S(2)}, u32[]{:S(2)}) collective-permute-start(bf16[1,45,256]{2,1,0:T(8,128)(2,1)} %get-tuple-element.36), channel_id=1, source_target_pairs={{0,8},{8,16},{16,24},{24,0},{1,9},{9,17},{17,25},{25,1},{2,10},{10... | collective-permute-start | bytes 69128 | tf_op jit(solution)/shard_map/ppermute | solution.py:15
  17.9 2.0 copy-start.2
  21.8 4.0 %copy-start.4 = (bf16[90,45,256]{2,1,0:T(8,128)(2,1)S(1)}, bf16[90,45,256]{2,1,0:T(8,128)(2,1)}, u32[]{:S(2)}) copy-start(bf16[90,45,256]{2,1,0:T(8,128)(2,1)} %param.7) | copy-start | bytes 6220804
  22.0 12.5 %copy-start = (bf16[92,45,256]{2,1,0:T(8,128)(2,1)}, bf16[92,45,256]{2,1,0:T(8,128)(2,1)S(1)}, u32[]{:S(2)}) copy-start(bf16[92,45,256]{2,1,0:T(8,128)(2,1)S(1)} %constant_dynamic-update-slice_fusion.4) | copy-start | bytes 6359044
  22.2 7.5 %collective-permute-start.7 = (bf16[92,1,256]{2,1,0:T(2,128)(2,1)S(1)}, bf16[92,1,256]{2,1,0:T(2,128)(2,1)S(1)}, u32[]{:S(2)}, u32[]{:S(2)}) collective-permute-start(bf16[92,1,256]{2,1,0:T(2,128)(2,1)S(1)} %get-tuple-element.31), channel_id=1, source_target_pairs={{0,1},{1,2},{2,3},{3,4},{4,5},{5,6},{6,7},{7,0},{8,9},{9,10},{10,1... | collective-permute-start | bytes 141320 | tf_op jit(solution)/shard_map/ppermute | solution.py:15
  22.2 7.5 %collective-permute-start.8 = (bf16[92,1,256]{2,1,0:T(2,128)(2,1)S(1)}, bf16[92,1,256]{2,1,0:T(2,128)(2,1)S(1)}, u32[]{:S(2)}, u32[]{:S(2)}) collective-permute-start(bf16[92,1,256]{2,1,0:T(2,128)(2,1)S(1)} %get-tuple-element.32), channel_id=1, source_target_pairs={{1,0},{2,1},{3,2},{4,3},{5,4},{6,5},{7,6},{0,7},{9,8},{10,9},{11,1... | collective-permute-start | bytes 141320 | tf_op jit(solution)/shard_map/ppermute | solution.py:17
  26.1 6.3 %collective-permute-start.2 = (bf16[92,1,256]{2,1,0:T(2,128)(2,1)S(1)}, bf16[92,1,256]{2,1,0:T(2,128)(2,1)S(1)}, u32[]{:S(2)}, u32[]{:S(2)}) collective-permute-start(bf16[92,1,256]{2,1,0:T(2,128)(2,1)S(1)} %get-tuple-element.33), channel_id=1, source_target_pairs={{0,1},{1,2},{2,3},{3,4},{4,5},{5,6},{6,7},{7,0},{8,9},{9,10},{10,1... | collective-permute-start | bytes 141320 | tf_op jit(solution)/shard_map/ppermute | solution.py:15
  26.2 6.2 %collective-permute-start.3 = (bf16[92,1,256]{2,1,0:T(2,128)(2,1)S(1)}, bf16[92,1,256]{2,1,0:T(2,128)(2,1)S(1)}, u32[]{:S(2)}, u32[]{:S(2)}) collective-permute-start(bf16[92,1,256]{2,1,0:T(2,128)(2,1)S(1)} %get-tuple-element.34), channel_id=1, source_target_pairs={{1,0},{2,1},{3,2},{4,3},{5,4},{6,5},{7,6},{0,7},{9,8},{10,9},{11,1... | collective-permute-start | bytes 141320 | tf_op jit(solution)/shard_map/ppermute | solution.py:17
  29.8 165.3 %collective-permute-start.9 = (bf16[2,47,256]{2,1,0:T(8,128)(2,1)S(1)}, bf16[2,47,256]{2,1,0:T(8,128)(2,1)S(1)}, u32[]{:S(2)}, u32[]{:S(2)}) collective-permute-start(bf16[2,47,256]{2,1,0:T(8,128)(2,1)S(1)} %fusion.57), channel_id=1, source_target_pairs={{0,4},{1,5},{2,6},{3,7},{4,0},{5,1},{6,2},{7,3},{8,12},{9,13},{10,... | collective-permute-start | bytes 144392 | tf_op jit(solution)/shard_map/ppermute | solution.py:27
  32.4 8.3 %collective-permute-start.4 = (bf16[2,47,256]{2,1,0:T(8,128)(2,1)S(1)}, bf16[2,47,256]{2,1,0:T(8,128)(2,1)S(1)}, u32[]{:S(2)}, u32[]{:S(2)}) collective-permute-start(bf16[2,47,256]{2,1,0:T(8,128)(2,1)S(1)} %fusion.54), channel_id=1, source_target_pairs={{0,4},{1,5},{2,6},{3,7},{4,0},{5,1},{6,2},{7,3},{8,12},{9,13},{10,... | collective-permute-start | bytes 144392 | tf_op jit(solution)/shard_map/ppermute | solution.py:27
  116.3 144.9 %all-reduce.5.cloned.1.call-start = ((), (), s32[]{:S(2)}) async-start(), calls=%async_computation.1 | async-start | bytes 4718592 | tf_op jit(solution)/shard_map/psum | solution.py:100
  116.4 2.7 %copy-start.1 = (bf16[92,45,256]{2,1,0:T(8,128)(2,1)S(1)}, bf16[92,45,256]{2,1,0:T(8,128)(2,1)}, u32[]{:S(2)}) copy-start(bf16[92,45,256]{2,1,0:T(8,128)(2,1)} %copy-done) | copy-start | bytes 6359044
  119.1 2.8 %copy-start.3 = (bf16[90,45,256]{2,1,0:T(8,128)(2,1)S(1)}, bf16[90,45,256]{2,1,0:T(8,128)(2,1)}, u32[]{:S(2)}) copy-start(bf16[90,45,256]{2,1,0:T(8,128)(2,1)} %param.9) | copy-start | bytes 6220804
  133.4 51.8 %copy-start.8 = (bf16[3,3,256,256]{2,3,1,0:T(8,128)(2,1)S(1)}, bf16[3,3,256,256]{2,3,1,0:T(8,128)(2,1)}, u32[]{:S(2)}) copy-start(bf16[3,3,256,256]{2,3,1,0:T(8,128)(2,1)} %rev.3) | copy-start | bytes 3538948
  185.2 9.9 %copy-start.6 = (bf16[1,3,256,256]{3,2,1,0:T(8,128)(2,1)S(1)}, bf16[1,3,256,256]{3,2,1,0:T(8,128)(2,1)}, u32[]{:S(2)}) copy-start(bf16[1,3,256,256]{3,2,1,0:T(8,128)(2,1)} %get-tuple-element.40) | copy-start | bytes 1179652
  185.2 10.2 %copy-start.5 = (bf16[1,3,256,256]{3,2,1,0:T(8,128)(2,1)S(1)}, bf16[1,3,256,256]{3,2,1,0:T(8,128)(2,1)}, u32[]{:S(2)}) copy-start(bf16[1,3,256,256]{3,2,1,0:T(8,128)(2,1)} %get-tuple-element.39) | copy-start | bytes 1179652
  195.5 1.6 copy-start.7
Sparse Core Ops, SparseCore 0:
  116.4 68.6 all-reduce.2
  188.3 72.8 all-reduce.4
where the time goes:
time: 272 us; the launch traced here: 271 us
  waiting for transfers between devices  107 us (39%)
  local copies, waits for them, and re-layouts  54.5 us (20%)
  other arithmetic  48.6 us (18%)
  matrix products  32.5 us (12%)
  starting transfers between devices  14.6 us (5%)
  between operations  14.3 us (5%)
    psum x1, waiting for transfers between devices, local(): summed = lax.psum(partial_sum, 'lat')  52.4 us
    psum x1, waiting for transfers between devices, local(): partial_sum = lax.psum(local_grad, 'lon')  51.7 us
    reshape x2, local copies, waits for them, and re-layouts, patches(): return jnp.concatenate(pieces, axis=-1).reshape(rows * cols, -1)  42.5 us
    unnamed x14, other arithmetic  34.7 us
    ppermute x4, starting transfers between devices, with_halo(): lax.ppermute(head, axis, [((i + 1) % count, i) for i in range(count)])  13.9 us
    dot_general x1, matrix products, local(): jnp.dot(columns, kernel.reshape(-1, width), preferred_element_type=jnp.fl...  11.6 us
    dot_general x1, matrix products, local(): lax.dot_general(columns, flat_grad, (((0,), (0,)), ((), ())), preferred_e...  10.6 us
    dot_general x1, matrix products, local(): jnp.dot(patches(padded_grad, rows, cols), flipped.reshape(-1, width), pre...  9.87 us
  transfers between devices with their start and end apart: 12, of which 3 were waited for; matrix products, arithmetic and copies ran while one was open for 48% of the time, Pallas kernels for 0%

commit v1 on v0

--- a/solution.py
+++ b/solution.py
@@ -3,6 +3,14 @@
 import jax.numpy as jnp
 from jax import lax
 from jax.sharding import PartitionSpec as P
+
+
+def added_up(value, mesh_axis):
+    size, result = (lax.axis_size(mesh_axis), value)
+    for far in [1 << k for k in range(size.bit_length() - 1)]:
+        swap = [(i, i ^ far) for i in range(size)]
+        result = result + lax.ppermute(result, mesh_axis, swap)
+    return result
 
 
 def with_halo(cells, sides, width):
@@ -97,7 +105,7 @@
     input_grad = input_grad.at[-1].add(jnp.where(south, south_term, 0.0))
     factor = 1.0 / math.sqrt(rows * cols * lax.axis_size("lat") * lax.axis_size("lon"))
     partial_sum = lax.psum(local_grad, "lon")
-    summed = lax.psum(partial_sum, "lat")
+    summed = added_up(partial_sum, "lat")
     return (outputs, input_grad.astype(jnp.bfloat16), summed * factor)
 
 

time: 272 us -> 286 us (1.051)
  local copies, waits for them, and re-layouts: 54.5 us -> 63 us
  other arithmetic: 48.6 us -> 51.8 us
  starting transfers between devices: 14.6 us -> 17.7 us
    psum x1 -> x0, waiting for transfers between devices: 52.4 us -> none  [local(): summed = lax.psum(partial_sum, 'lat')]
    ppermute x0 -> x2, waiting for transfers between devices: none -> 41.6 us  [added_up(): result = result + lax.ppermute(result, mesh_axis, swap)]
    psum x1, waiting for transfers between devices: 51.7 us -> 57.1 us  [local(): partial_sum = lax.psum(local_grad, 'lon')]
    ppermute x4, starting transfers between devices: 13.9 us -> 9.99 us  [with_halo(): lax.ppermute(head, axis, [((i + 1) % count, i) for i in range(count)])]
    ppermute x4, starting transfers between devices: 0.12 us -> 3.13 us  [with_halo(): lax.ppermute(tail, axis, [(i, (i + 1) % count) for i in range(count)])]
    ppermute x0 -> x2, starting transfers between devices: none -> 2.98 us  [added_up(): result = result + lax.ppermute(result, mesh_axis, swap)]
  transfers between devices with their start and end apart: 12 -> 13, of which waited for: 3 -> 7; matrix products, arithmetic and copies ran while one was open for 48% -> 24% of each run, Pallas kernels for 0% -> 0%
where the time goes in v1:
time: 286 us; the launch traced here: 285 us
  waiting for transfers between devices  106 us (37%)
  local copies, waits for them, and re-layouts  63 us (22%)
  other arithmetic  51.8 us (18%)
  matrix products  32.2 us (11%)
  starting transfers between devices  17.7 us (6%)
  between operations  14.2 us (5%)
    psum x1, waiting for transfers between devices, local(): partial_sum = lax.psum(local_grad, 'lon')  57.1 us
    reshape x2, local copies, waits for them, and re-layouts, patches(): return jnp.concatenate(pieces, axis=-1).reshape(rows * cols, -1)  44.3 us
    ppermute x2, waiting for transfers between devices, added_up(): result = result + lax.ppermute(result, mesh_axis, swap)  41.6 us
    unnamed x14, other arithmetic  35.6 us
    dot_general x1, matrix products, local(): jnp.dot(columns, kernel.reshape(-1, width), preferred_element_type=jnp.fl...  11.5 us
    dot_general x1, matrix products, local(): lax.dot_general(columns, flat_grad, (((0,), (0,)), ((), ())), preferred_e...  10.4 us
    ppermute x4, starting transfers between devices, with_halo(): lax.ppermute(head, axis, [((i + 1) % count, i) for i in range(count)])  9.99 us
    dot_general x1, matrix products, local(): jnp.dot(patches(padded_grad, rows, cols), flipped.reshape(-1, width), pre...  9.85 us
  transfers between devices with their start and end apart: 13, of which 7 were waited for; matrix products, arithmetic and copies ran while one was open for 24% of the time, Pallas kernels for 0%

profile of v1, /device:TPU:0, one launch (start us, length us, event | category | flops | bytes accessed | tf_op | source)
XLA Modules:
  0.0 284.9 jit_solution(6198679087887600608)
XLA Ops:
  7.2 0.0 all-reduce.2.cloned.1.call-start
  7.2 0.8 fusion.70
  8.0 3.0 %collective-permute-start = (bf16[1,45,256]{2,1,0:T(8,128)(2,1)S(1)}, bf16[1,45,256]{2,1,0:T(8,128)(2,1)S(1)}, u32[]{:S(2)}, u32[]{:S(2)}) collective-permute-start(bf16[1,45,256]{2,1,0:T(8,128)(2,1)S(1)} %get-tuple-element.38), channel_id=1, source_target_pairs={{0,8},{8,16},{16,24},{24,0},{1,9},{9,17},{17,25},{25,1},{2,10},{10... | collective-permute-start | bytes 69128 | tf_op jit(solution)/shard_map/ppermute | solution.py:23
  10.9 1.0 collective-permute-start.1
  11.9 1.8 collective-permute-done
  13.7 1.8 constant_dynamic-update-slice_fusion.1
  15.5 0.1 fusion.68
  15.7 0.1 collective-permute-start.2
  15.7 3.5 %collective-permute-start.3 = (bf16[92,1,256]{2,1,0:T(2,128)(2,1)S(1)}, bf16[92,1,256]{2,1,0:T(2,128)(2,1)S(1)}, u32[]{:S(2)}, u32[]{:S(2)}) collective-permute-start(bf16[92,1,256]{2,1,0:T(2,128)(2,1)S(1)} %get-tuple-element.34), channel_id=1, source_target_pairs={{1,0},{2,1},{3,2},{4,3},{5,4},{6,5},{7,6},{0,7},{9,8},{10,9},{11,1... | collective-permute-start | bytes 141320 | tf_op jit(solution)/shard_map/ppermute | solution.py:25
  19.2 4.0 %reshape.103 = bf16[4050,256,1,1]{1,0,2,3:T(8,128)(2,1)} reshape(bf16[90,45,256]{2,1,0:T(8,128)(2,1)} %param.9) | data formatting | bytes 4147200 | tf_op jit(solution)/shard_map/reshape | solution.py:79
  23.3 1.5 collective-permute-start.4
  24.7 1.5 pad_maximum_fusion
  26.3 0.1 slice.283
  26.4 2.3 collective-permute-done.4
  28.7 1.7 fusion.15
  30.4 2.8 %fusion.13 = bf16[90,45,2304]{2,1,0:T(8,128)(2,1)} fusion(bf16[90,45,2304]{2,1,0:T(8,128)(2,1)} %fusion.15, bf16[1,47,256]{2,1,0:T(8,128)(2,1)S(1)} %get-tuple-element.28, bf16[90,47,256]{2,1,0:T(8,128)(2,1)S(1)} %slice.283), kind=kLoop, calls=%fused_computation.24 | loop fusion | flops 4147200 | bytes 4401664
  33.3 2.8 fusion.23
  36.0 2.9 %fusion.22 = bf16[90,45,2304]{2,1,0:T(8,128)(2,1)} fusion(bf16[90,45,2304]{2,1,0:T(8,128)(2,1)} %fusion.23, bf16[92,45,256]{2,1,0:T(8,128)(2,1)S(1)} %constant_dynamic-update-slice_fusion, bf16[92,1,256]{2,1,0:T(2,128)(2,1)S(1)} %collective-permute-done.2), kind=kLoop, calls=%fused_computation.40 | loop fusion | flops 4147200 | bytes 4378624
  38.9 1.7 constant_dynamic-update-slice_fusion.3
  40.7 2.9 %fusion.21 = bf16[90,45,2304]{2,1,0:T(8,128)(2,1)} fusion(bf16[90,45,2304]{2,1,0:T(8,128)(2,1)} %constant_dynamic-update-slice_fusion.3, bf16[92,1,256]{2,1,0:T(2,128)(2,1)S(1)} %collective-permute-done.3, bf16[92,45,256]{2,1,0:T(8,128)(2,1)S(1)} %constant_dynamic-update-slice_fusion), kind=kLoop, calls=%fused_computation.38 | loop fusion | flops 4147200 | bytes 4378624
  43.6 1.6 fusion.11
  45.2 2.9 %fusion.9 = bf16[90,45,2304]{2,1,0:T(8,128)(2,1)} fusion(bf16[90,45,2304]{2,1,0:T(8,128)(2,1)} %fusion.11, bf16[1,47,256]{2,1,0:T(8,128)(2,1)S(1)} %get-tuple-element.27, bf16[90,47,256]{2,1,0:T(8,128)(2,1)S(1)} %slice.283), kind=kLoop, calls=%fused_computation.20 | loop fusion | flops 4147200 | bytes 4401664
  48.1 2.8 fusion.20
  50.9 19.4 %reshape.99 = bf16[4050,2304]{1,0:T(8,128)(2,1)} reshape(bf16[90,45,2304]{2,1,0:T(8,128)(2,1)} %fusion.20) | data formatting | bytes 37324800 | tf_op jit(solution)/shard_map/reshape | solution.py:44
  70.3 24.9 %copy.7 = bf16[4050,2304]{0,1:T(8,128)(2,1)} copy(bf16[4050,2304]{1,0:T(8,128)(2,1)} %reshape.99) | data formatting | bytes 37324800 | tf_op jit(solution)/shard_map/reshape | solution.py:44
  95.2 10.4 %fusion.24 = f32[3,3,256,256]{3,2,1,0:T(8,128)} fusion(bf16[3,3,256,4050]{3,2,1,0:T(8,128)(2,1)} %bitcast.46, bf16[4050,256,1,1]{1,0,2,3:T(8,128)(2,1)S(1)} %copy-done.3), kind=kOutput, calls=%fused_computation.43 | convolution fusion | flops 4777574400 | bytes 23095296 | tf_op jit(solution)/shard_map/dot_general | solution.py:80
  105.6 0.9 fusion.69
  106.5 1.9 collective-permute-start.6
  108.4 0.1 collective-permute-start.5
  108.5 0.7 copy.6
  109.2 1.1 reverse_bitcast_fusion
  110.3 2.8 collective-permute-done.5
  113.1 1.8 constant_dynamic-update-slice_fusion.5
  114.9 57.1 %all-reduce.2.cloned.1.call-done = f32[3,3,256,256]{3,2,1,0:T(8,128)} async-done(((f32[3,3,256,256]{3,2,1,0:T(8,128)}), f32[3,3,256,256]{3,2,1,0:T(8,128)}) %all-reduce.2.cloned.1.call-update) | async-done | bytes 2359312 | tf_op jit(solution)/shard_map/psum | solution.py:107
  172.0 1.5 collective-permute-start.10
  173.5 0.8 fusion.67
  174.3 3.5 %collective-permute-start.8 = (bf16[92,1,256]{2,1,0:T(2,128)(2,1)}, bf16[92,1,256]{2,1,0:T(2,128)(2,1)S(1)}, u32[]{:S(2)}, u32[]{:S(2)}) collective-permute-start(bf16[92,1,256]{2,1,0:T(2,128)(2,1)} %get-tuple-element.32), channel_id=1, source_target_pairs={{1,0},{2,1},{3,2},{4,3},{5,4},{6,5},{7,6},{0,7},{9,8},{10,9},{11,1... | collective-permute-start | bytes 141320 | tf_op jit(solution)/shard_map/ppermute | solution.py:25
  177.8 2.0 fusion.71
  179.9 1.1 rev.3
  181.0 0.4 collective-permute-done.7
  181.4 0.7 fusion.57
  182.1 0.1 collective-permute-start.9
  182.2 2.3 pad_maximum_fusion.1
  184.5 0.1 slice.295
  184.6 0.7 maximum_select_fusion
  185.3 1.6 fusion.7
  186.9 2.7 fusion.5
  189.6 2.7 fusion.19
  192.4 3.6 %fusion.18 = bf16[90,45,2304]{2,1,0:T(8,128)(2,1)} fusion(bf16[90,45,2304]{2,1,0:T(8,128)(2,1)} %fusion.19, bf16[92,45,256]{2,1,0:T(8,128)(2,1)S(1)} %constant_dynamic-update-slice_fusion.4, bf16[92,1,256]{2,1,0:T(2,128)(2,1)} %collective-permute-done.7), kind=kLoop, calls=%fused_computation.32 | loop fusion | flops 4147200 | bytes 4425728
  196.0 1.6 constant_dynamic-update-slice_fusion.7
  197.6 3.0 %fusion.17 = bf16[90,45,2304]{2,1,0:T(8,128)(2,1)} fusion(bf16[90,45,2304]{2,1,0:T(8,128)(2,1)} %constant_dynamic-update-slice_fusion.7, bf16[92,1,256]{2,1,0:T(2,128)(2,1)S(1)} %collective-permute-done.8, bf16[92,45,256]{2,1,0:T(8,128)(2,1)S(1)} %constant_dynamic-update-slice_fusion.4), kind=kLoop, calls=%fused_computation.30 | loop fusion | flops 4147200 | bytes 4378624
  200.6 1.6 fusion.3
  202.2 2.7 fusion.1
  204.9 2.8 fusion.16
  207.7 16.1 %collective-permute-done.10 = f32[3,3,256,256]{3,2,1,0:T(8,128)} collective-permute-done((f32[3,3,256,256]{3,2,1,0:T(8,128)}, f32[3,3,256,256]{3,2,1,0:T(8,128)}, u32[]{:S(2)}, u32[]{:S(2)}) %collective-permute-start.10) | collective-permute-done | bytes 2359328 | tf_op jit(solution)/shard_map/ppermute | solution.py:12
  223.7 2.0 add.24
  225.7 1.5 collective-permute-start.11
  227.2 9.8 %fusion.72 = f32[90,45,256]{2,1,0:T(8,128)S(1)} fusion(bf16[90,45,2304]{2,1,0:T(8,128)(2,1)} %fusion.16, bf16[2304,256,1]{1,0,2:T(8,128)(2,1)S(1)} %bitcast.50), kind=kOutput, calls=%fused_computation.114 | convolution fusion | flops 4777574400 | bytes 23989248 | tf_op jit(solution)/shard_map/dot_general | solution.py:96
  237.1 0.2 fusion.62
  237.4 0.2 fusion.28
  237.6 1.6 convert_element_type.7
  239.2 11.5 %convolution_convert_fusion = bf16[90,45,256]{2,1,0:T(8,128)(2,1)} fusion(bf16[90,45,2304]{2,1,0:T(8,128)(2,1)} %fusion.20, bf16[2304,256,1]{1,0,2:T(8,128)(2,1)S(1)} %bitcast.49), kind=kOutput, calls=%fused_computation.45 | convolution fusion | flops 4778611200 | bytes 21915648 | tf_op jit(solution)/shard_map/dot_general | solution.py:77
  250.7 25.6 %collective-permute-done.11 = f32[3,3,256,256]{3,2,1,0:T(8,128)S(1)} collective-permute-done((f32[3,3,256,256]{3,2,1,0:T(8,128)S(1)}, f32[3,3,256,256]{3,2,1,0:T(8,128)S(1)}, u32[]{:S(2)}, u32[]{:S(2)}) %collective-permute-start.11) | collective-permute-done | bytes 2359328 | tf_op jit(solution)/shard_map/ppermute | solution.py:12
  276.3 1.7 add_multiply_fusion
  (33 shorter events, 0.2 us)
Async XLA Ops:
  7.2 164.9 %all-reduce.2.cloned.1.call-start = ((), (), s32[]{:S(2)}) async-start(), calls=%async_computation | async-start | bytes 4718592 | tf_op jit(solution)/shard_map/psum | solution.py:107
  8.0 5.7 %collective-permute-start = (bf16[1,45,256]{2,1,0:T(8,128)(2,1)S(1)}, bf16[1,45,256]{2,1,0:T(8,128)(2,1)S(1)}, u32[]{:S(2)}, u32[]{:S(2)}) collective-permute-start(bf16[1,45,256]{2,1,0:T(8,128)(2,1)S(1)} %get-tuple-element.38), channel_id=1, source_target_pairs={{0,8},{8,16},{16,24},{24,0},{1,9},{9,17},{17,25},{25,1},{2,10},{10... | collective-permute-start | bytes 69128 | tf_op jit(solution)/shard_map/ppermute | solution.py:23
  10.9 4.5 %collective-permute-start.1 = (bf16[1,45,256]{2,1,0:T(8,128)(2,1)S(1)}, bf16[1,45,256]{2,1,0:T(8,128)(2,1)S(1)}, u32[]{:S(2)}, u32[]{:S(2)}) collective-permute-start(bf16[1,45,256]{2,1,0:T(8,128)(2,1)S(1)} %get-tuple-element.37), channel_id=1, source_target_pairs={{8,0},{16,8},{24,16},{0,24},{9,1},{17,9},{25,17},{1,25},{10,2},{18... | collective-permute-start | bytes 69128 | tf_op jit(solution)/shard_map/ppermute | solution.py:25
  15.7 7.6 %collective-permute-start.2 = (bf16[92,1,256]{2,1,0:T(2,128)(2,1)S(1)}, bf16[92,1,256]{2,1,0:T(2,128)(2,1)S(1)}, u32[]{:S(2)}, u32[]{:S(2)}) collective-permute-start(bf16[92,1,256]{2,1,0:T(2,128)(2,1)S(1)} %get-tuple-element.33), channel_id=1, source_target_pairs={{0,1},{1,2},{2,3},{3,4},{4,5},{5,6},{6,7},{7,0},{8,9},{9,10},{10,1... | collective-permute-start | bytes 141320 | tf_op jit(solution)/shard_map/ppermute | solution.py:23
  15.7 7.5 %collective-permute-start.3 = (bf16[92,1,256]{2,1,0:T(2,128)(2,1)S(1)}, bf16[92,1,256]{2,1,0:T(2,128)(2,1)S(1)}, u32[]{:S(2)}, u32[]{:S(2)}) collective-permute-start(bf16[92,1,256]{2,1,0:T(2,128)(2,1)S(1)} %get-tuple-element.34), channel_id=1, source_target_pairs={{1,0},{2,1},{3,2},{4,3},{5,4},{6,5},{7,6},{0,7},{9,8},{10,9},{11,1... | collective-permute-start | bytes 141320 | tf_op jit(solution)/shard_map/ppermute | solution.py:25
  23.3 5.4 %collective-permute-start.4 = (bf16[2,47,256]{2,1,0:T(8,128)(2,1)S(1)}, bf16[2,47,256]{2,1,0:T(8,128)(2,1)S(1)}, u32[]{:S(2)}, u32[]{:S(2)}) collective-permute-start(bf16[2,47,256]{2,1,0:T(8,128)(2,1)S(1)} %fusion.54), channel_id=1, source_target_pairs={{0,4},{1,5},{2,6},{3,7},{4,0},{5,1},{6,2},{7,3},{8,12},{9,13},{10,... | collective-permute-start | bytes 144392 | tf_op jit(solution)/shard_map/ppermute | solution.py:35
  36.0 2.9 %copy-start.1 = (bf16[90,45,256]{2,1,0:T(8,128)(2,1)S(1)}, bf16[90,45,256]{2,1,0:T(8,128)(2,1)}, u32[]{:S(2)}) copy-start(bf16[90,45,256]{2,1,0:T(8,128)(2,1)} %param.7) | copy-start | bytes 6220804
  70.3 24.9 %copy-start.3 = (bf16[4050,256,1,1]{1,0,2,3:T(8,128)(2,1)S(1)}, bf16[4050,256,1,1]{1,0,2,3:T(8,128)(2,1)}, u32[]{:S(2)}) copy-start(bf16[4050,256,1,1]{1,0,2,3:T(8,128)(2,1)} %reshape.103) | copy-start | bytes 6220804
  105.6 2.9 %copy-start.6 = (bf16[3,3,256,256]{3,2,1,0:T(8,128)(2,1)S(1)}, bf16[3,3,256,256]{3,2,1,0:T(8,128)(2,1)}, u32[]{:S(2)}) copy-start(bf16[3,3,256,256]{3,2,1,0:T(8,128)(2,1)} %param.8) | copy-start | bytes 3538948
  106.5 8.4 %collective-permute-start.6 = (bf16[1,45,256]{2,1,0:T(8,128)(2,1)S(1)}, bf16[1,45,256]{2,1,0:T(8,128)(2,1)S(1)}, u32[]{:S(2)}, u32[]{:S(2)}) collective-permute-start(bf16[1,45,256]{2,1,0:T(8,128)(2,1)S(1)} %get-tuple-element.35), channel_id=1, source_target_pairs={{8,0},{16,8},{24,16},{0,24},{9,1},{17,9},{25,17},{1,25},{10,2},{18... | collective-permute-start | bytes 69128 | tf_op jit(solution)/shard_map/ppermute | solution.py:25
  108.4 4.7 %collective-permute-start.5 = (bf16[1,45,256]{2,1,0:T(8,128)(2,1)S(1)}, bf16[1,45,256]{2,1,0:T(8,128)(2,1)S(1)}, u32[]{:S(2)}, u32[]{:S(2)}) collective-permute-start(bf16[1,45,256]{2,1,0:T(8,128)(2,1)S(1)} %get-tuple-element.36), channel_id=1, source_target_pairs={{0,8},{8,16},{16,24},{24,0},{1,9},{9,17},{17,25},{25,1},{2,10},{10... | collective-permute-start | bytes 69128 | tf_op jit(solution)/shard_map/ppermute | solution.py:23
  172.0 51.7 %collective-permute-start.10 = (f32[3,3,256,256]{3,2,1,0:T(8,128)}, f32[3,3,256,256]{3,2,1,0:T(8,128)}, u32[]{:S(2)}, u32[]{:S(2)}) collective-permute-start(f32[3,3,256,256]{3,2,1,0:T(8,128)} %all-reduce.2.cloned.1.call-done), channel_id=1, source_target_pairs={{0,8},{8,0},{16,24},{24,16},{1,9},{9,1},{17,25},{25,17},{2,10},{10... | collective-permute-start | bytes 7077896 | tf_op jit(solution)/shard_map/ppermute | solution.py:12
  174.3 7.1 %collective-permute-start.7 = (bf16[92,1,256]{2,1,0:T(2,128)(2,1)}, bf16[92,1,256]{2,1,0:T(2,128)(2,1)}, u32[]{:S(2)}, u32[]{:S(2)}) collective-permute-start(bf16[92,1,256]{2,1,0:T(2,128)(2,1)} %get-tuple-element.31), channel_id=1, source_target_pairs={{0,1},{1,2},{2,3},{3,4},{4,5},{5,6},{6,7},{7,0},{8,9},{9,10},{10,1... | collective-permute-start | bytes 141320 | tf_op jit(solution)/shard_map/ppermute | solution.py:23
  174.3 7.1 %collective-permute-start.8 = (bf16[92,1,256]{2,1,0:T(2,128)(2,1)}, bf16[92,1,256]{2,1,0:T(2,128)(2,1)S(1)}, u32[]{:S(2)}, u32[]{:S(2)}) collective-permute-start(bf16[92,1,256]{2,1,0:T(2,128)(2,1)} %get-tuple-element.32), channel_id=1, source_target_pairs={{1,0},{2,1},{3,2},{4,3},{5,4},{6,5},{7,6},{0,7},{9,8},{10,9},{11,1... | collective-permute-start | bytes 141320 | tf_op jit(solution)/shard_map/ppermute | solution.py:25
  182.1 55.0 %collective-permute-start.9 = (bf16[2,47,256]{2,1,0:T(8,128)(2,1)S(1)}, bf16[2,47,256]{2,1,0:T(8,128)(2,1)S(1)}, u32[]{:S(2)}, u32[]{:S(2)}) collective-permute-start(bf16[2,47,256]{2,1,0:T(8,128)(2,1)S(1)} %fusion.57), channel_id=1, source_target_pairs={{0,4},{1,5},{2,6},{3,7},{4,0},{5,1},{6,2},{7,3},{8,12},{9,13},{10,... | collective-permute-start | bytes 144392 | tf_op jit(solution)/shard_map/ppermute | solution.py:35
  192.4 3.6 %copy-start = (bf16[90,45,256]{2,1,0:T(8,128)(2,1)S(1)}, bf16[90,45,256]{2,1,0:T(8,128)(2,1)}, u32[]{:S(2)}) copy-start(bf16[90,45,256]{2,1,0:T(8,128)(2,1)} %param.9) | copy-start | bytes 6220804
  204.9 18.8 %copy-start.2 = (f32[3,3,256,256]{3,2,1,0:T(8,128)S(1)}, f32[3,3,256,256]{3,2,1,0:T(8,128)}, u32[]{:S(2)}) copy-start(f32[3,3,256,256]{3,2,1,0:T(8,128)} %all-reduce.2.cloned.1.call-done) | copy-start | bytes 7077892
  207.7 19.6 %copy-start.8 = (bf16[3,3,256,256]{2,3,1,0:T(8,128)(2,1)S(1)}, bf16[3,3,256,256]{2,3,1,0:T(8,128)(2,1)}, u32[]{:S(2)}) copy-start(bf16[3,3,256,256]{2,3,1,0:T(8,128)(2,1)} %rev.3) | copy-start | bytes 3538948
  225.7 50.6 %collective-permute-start.11 = (f32[3,3,256,256]{3,2,1,0:T(8,128)S(1)}, f32[3,3,256,256]{3,2,1,0:T(8,128)S(1)}, u32[]{:S(2)}, u32[]{:S(2)}) collective-permute-start(f32[3,3,256,256]{3,2,1,0:T(8,128)S(1)} %add.24), channel_id=1, source_target_pairs={{0,16},{8,24},{16,0},{24,8},{1,17},{9,25},{17,1},{25,9},{2,18},{10... | collective-permute-start | bytes 7077896 | tf_op jit(solution)/shard_map/ppermute | solution.py:12
  227.2 9.9 %copy-start.5 = (bf16[1,3,256,256]{3,2,1,0:T(8,128)(2,1)S(1)}, bf16[1,3,256,256]{3,2,1,0:T(8,128)(2,1)}, u32[]{:S(2)}) copy-start(bf16[1,3,256,256]{3,2,1,0:T(8,128)(2,1)} %get-tuple-element.40) | copy-start | bytes 1179652
  227.2 10.1 %copy-start.4 = (bf16[1,3,256,256]{3,2,1,0:T(8,128)(2,1)S(1)}, bf16[1,3,256,256]{3,2,1,0:T(8,128)(2,1)}, u32[]{:S(2)}) copy-start(bf16[1,3,256,256]{3,2,1,0:T(8,128)(2,1)} %get-tuple-element.39) | copy-start | bytes 1179652
  237.6 1.6 copy-start.7
Sparse Core Ops, SparseCore 0:
  105.7 66.2 all-reduce.1
